TPU v7x, 32 devices: a whole 2x2x4 slice. The times are simulated.
32 devices in a mesh: ctx: 16 (over z, y, x), ch: 2 (over core).
Axes of the slice: x: 2, y: 2, z: 4, core: 2. Of those that a mesh axis runs over, the one named last changes fastest.
Arguments:
- tokens: bfloat16 [16384, 8192], P('ctx', 'ch'), may hold values from -6 to 6
- in_weight: bfloat16 [128, 3, 8192], P('ctx', None, 'ch'), may hold values from -0.09375 to 0.09375
- conv_filter: float32 [128, 16384], P('ch', 'ctx'), as said below
- skip_gain: float32 [128], P('ch'), may hold values from -4 to 4
- group_order: int32 [32], replicated, may hold values from 0 to 31, each once
- out_weight: bfloat16 [128, 8192], P('ctx', 'ch'), may hold values from -0.5 to 0.5
Outputs:
- mixed: bfloat16 [16384, 8192], P('ctx', 'ch')
Inputs may be any that keep to these rules, and one draw needn't show every extreme that they name: `conv_filter`: each channel's filter has a sum of squares of one over all 16384 lags. `group_order`: a permutation of the storage blocks' group numbers.
All inputs are finite; a program needn't handle non-finite values.
Results may differ from a plain program's by a relative error of at most 0.0049.
Values may be sent and summed in bfloat16 or wider, within the bound.
A program may use at most 192 MiB of HBM per device.

v0:
```python
import math

import jax
import jax.numpy as jnp
from jax import lax
from jax.sharding import PartitionSpec as P

highest = lax.Precision.HIGHEST


def angle_table(row_ids, col_ids, period):
    phase = row_ids[:, None] * col_ids[None, :] % period
    return phase.astype(jnp.float32) * (2.0 * math.pi / period)


def to_blocks(signal, ctx_count):
    chan_local, tok_count = signal.shape
    per_peer = tok_count // (2 * ctx_count)
    moved = signal.reshape(chan_local, 2, ctx_count, per_peer).transpose(1, 2, 0, 3)
    return moved.reshape(2, ctx_count, chan_local * per_peer)


def block_section(received, theta, phi, ctx_count):
    values = received.reshape(theta.shape[1], -1)
    real_part = jnp.dot(jnp.cos(theta), values, precision=highest)
    imag_part = -jnp.dot(jnp.sin(theta), values, precision=highest)
    cos_phi = jnp.cos(phi)
    sin_phi = jnp.sin(phi)
    twist_real = real_part * cos_phi + imag_part * sin_phi
    twist_imag = imag_part * cos_phi - real_part * sin_phi
    return jnp.stack([twist_real, twist_imag]).reshape(2, 4, ctx_count, values.shape[1])


def freq_section(received, cos_b, sin_b, chan_local):
    ctx_count = cos_b.shape[1]
    per_peer = cos_b.shape[2]
    values = received.reshape(2, 4, ctx_count, chan_local, per_peer)
    real_in = values[0]
    imag_in = values[1]
    real_part = jnp.einsum("recb,keb->rck", real_in, cos_b, precision=highest) + jnp.einsum(
        "recb,keb->rck", imag_in, sin_b, precision=highest
    )
    imag_part = jnp.einsum("recb,keb->rck", imag_in, cos_b, precision=highest) - jnp.einsum(
        "recb,keb->rck", real_in, sin_b, precision=highest
    )
    return (real_part, imag_part)


def per_device(tokens, in_weight, conv_filter, skip_gain, group_order, out_weight):
    ctx_count = lax.axis_size("ctx")
    own_index = lax.axis_index("ctx")
    tok_count, feat_local = tokens.shape
    chan_local = conv_filter.shape[0]
    per_peer = tok_count // (2 * ctx_count)
    group = tok_count // 2
    block_count = 2 * ctx_count
    freq_count = 4 * ctx_count
    width = chan_local * per_peer
    total_length = freq_count * group
    weights_all = lax.all_gather(in_weight, "ctx", axis=0, tiled=True)
    chans = weights_all.shape[0]
    flat = weights_all.reshape(chans * 3, feat_local)
    proj = lax.psum_scatter(
        lax.dot_general(flat, tokens, (((1,), (1,)), ((), ())), preferred_element_type=jnp.float32),
        "ch",
        scatter_dimension=0,
        tiled=True,
    )
    proj = proj.reshape(chan_local, 3, tok_count)
    gate_part = proj[:, 0]
    key_part = proj[:, 1]
    value_part = proj[:, 2]
    product = key_part * value_part
    freq_ids = jnp.arange(freq_count, dtype=jnp.int32)
    theta_signal = angle_table(freq_ids, group_order, freq_count)
    theta_filter = angle_table(freq_ids, jnp.arange(block_count, dtype=jnp.int32), freq_count)
    offsets = own_index * per_peer + jnp.arange(width, dtype=jnp.int32) % per_peer
    phi = angle_table(freq_ids, offsets, total_length)
    inner_ids = jnp.arange(group, dtype=jnp.int32)
    psi = angle_table(inner_ids, inner_ids, group).reshape(group, ctx_count, per_peer)
    cos_b = jnp.cos(psi)
    sin_b = jnp.sin(psi)
    signal_parts = to_blocks(product, ctx_count)
    filter_parts = to_blocks(conv_filter, ctx_count)
    filter_recv = lax.all_to_all(filter_parts, "ctx", split_axis=1, concat_axis=0, tiled=True)
    filter_freq = lax.all_to_all(
        block_section(filter_recv, theta_filter, phi, ctx_count),
        "ctx",
        split_axis=2,
        concat_axis=3,
        tiled=True,
    )
    signal_recv = lax.all_to_all(signal_parts, "ctx", split_axis=1, concat_axis=0, tiled=True)
    signal_freq = lax.all_to_all(
        block_section(signal_recv, theta_signal, phi, ctx_count),
        "ctx",
        split_axis=2,
        concat_axis=3,
        tiled=True,
    )
    signal_real, signal_imag = freq_section(signal_freq, cos_b, sin_b, chan_local)
    filter_real, filter_imag = freq_section(filter_freq, cos_b, sin_b, chan_local)
    spec_real = signal_real * filter_real - signal_imag * filter_imag
    spec_imag = signal_real * filter_imag + signal_imag * filter_real
    back_real = jnp.einsum("rck,keb->recb", spec_real, cos_b, precision=highest) - jnp.einsum(
        "rck,keb->recb", spec_imag, sin_b, precision=highest
    )
    back_imag = jnp.einsum("rck,keb->recb", spec_imag, cos_b, precision=highest) + jnp.einsum(
        "rck,keb->recb", spec_real, sin_b, precision=highest
    )
    stacked = jnp.stack([back_real, back_imag]).reshape(2, 4, 1, ctx_count * width)
    returned = lax.all_to_all(stacked, "ctx", split_axis=3, concat_axis=2, tiled=True).reshape(
        2, freq_count, width
    )
    cos_phi = jnp.cos(phi)
    sin_phi = jnp.sin(phi)
    turned_real = returned[0] * cos_phi - returned[1] * sin_phi
    turned_imag = returned[0] * sin_phi + returned[1] * cos_phi
    block_values = jnp.dot(jnp.cos(theta_signal).T, turned_real, precision=highest) - jnp.dot(
        jnp.sin(theta_signal).T, turned_imag, precision=highest
    )
    block_values = block_values * (1.0 / total_length)
    arrived = lax.all_to_all(
        block_values.reshape(block_count, 1, width), "ctx", split_axis=0, concat_axis=1, tiled=True
    )
    conv = (
        arrived.reshape(2, ctx_count, chan_local, per_peer)
        .transpose(2, 0, 1, 3)
        .reshape(chan_local, tok_count)
    )
    hidden = (gate_part * (conv + skip_gain[:, None] * product)).astype(jnp.bfloat16)
    hidden_all = lax.all_gather(hidden, "ch", axis=0, tiled=True)
    rows_all = lax.all_gather(out_weight, "ctx", axis=0, tiled=True)
    mixed = lax.dot_general(
        hidden_all, rows_all, (((0,), (0,)), ((), ())), preferred_element_type=jnp.float32
    )
    return mixed.astype(jnp.bfloat16)


def solution(mesh):
    in_specs = (P("ctx", "ch"), P("ctx", None, "ch"), P("ch", "ctx"), P("ch"), P(), P("ctx", "ch"))
    out_specs = P("ctx", "ch")
    return jax.shard_map(
        per_device, mesh=mesh, in_specs=in_specs, out_specs=out_specs, check_vma=False
    )
```

profile of v0, /device:TPU:0, one launch (start us, length us, event | category | flops | bytes accessed | tf_op | source)
XLA Modules:
  0.0 721.7 jit_solution(2608956717832617724)
XLA Ops:
  7.3 73.4 %all-gather.3.cloned.1.call-done = bf16[128,3,4096]{2,0,1:T(8,128)(2,1)} async-done(((bf16[8,3,4096]{2,0,1:T(8,128)(2,1)}), bf16[128,3,4096]{2,0,1:T(8,128)(2,1)}) %all-gather.3.cloned.1.call-update) | async-done | bytes 3145744 | tf_op jit(solution)/shard_map/all_gather | solution.py:60
  80.7 6.6 copy.30
  87.3 6.0 reshape.111
  93.3 7.0 fusion.177
  100.9 1.3 reshape.134
  102.2 4.2 all-to-all-start.2
  106.5 1.7 reduce-scatter.2.cloned.1.call-done
  108.2 1.5 reshape.112
  111.4 1.3 reshape.133
  112.7 3.1 all-to-all-done.2
  115.8 4.1 all-to-all-start
  120.7 9.3 %all-to-all-done = f32[2,16,2048]{2,0,1:T(2,128)S(1)} async-done(((f32[2,16,2048]{2,0,1:T(2,128)}), f32[2,16,2048]{2,0,1:T(2,128)S(1)}, u32[]{:S(2)}, u32[]{:S(2)}) %all-to-all-start) | async-done | bytes 262176 | tf_op jit(solution)/shard_map/all_to_all | solution.py:93
  131.6 2.8 multiply_add_fusion.1
  136.4 3.7 all-to-all-start.3
  140.7 1.3 pad_maximum_fusion
  142.0 21.9 %all-to-all-done.3 = f32[2,4,16,2048]{3,1,0,2:T(4,128)S(1)} async-done(((f32[2,4,16,2048]{3,1,0,2:T(4,128)}), f32[2,4,16,2048]{3,1,0,2:T(4,128)S(1)}, u32[]{:S(2)}, u32[]{:S(2)}) %all-to-all-start.3) | async-done | bytes 1048608 | tf_op jit(solution)/shard_map/all_to_all | solution.py:86
  163.9 6.3 all-to-all-start.1
  170.6 2.0 squeeze.28
  172.9 2.0 squeeze.29
  175.0 7.7 %convolution_bitcast_fusion = f32[4,64,512]{2,1,0:T(8,128)S(1)} fusion(f32[4,16,64,32]{3,2,1,0:T(8,128)} %squeeze.28, s32[16,32]{1,0:T(8,128)S(1)} %multiply_add_fusion.3), kind=kOutput, calls=%fused_computation.13 | convolution fusion | flops 808976384 | bytes 1050624 | tf_op jit(solution)/shard_map/recb,keb->rck/dot_general | solution.py:43
  182.7 6.9 convolution_bitcast_fusion.4
  189.6 6.7 fusion.7
  197.5 7.0 convolution_bitcast_fusion.6
  204.8 2.0 squeeze.26
  206.8 7.7 %convolution_bitcast_fusion.2 = f32[4,64,512]{2,1,0:T(8,128)S(1)} fusion(f32[4,16,64,32]{3,2,1,0:T(8,128)} %squeeze.26, s32[16,32]{1,0:T(8,128)S(1)} %multiply_add_fusion.3), kind=kOutput, calls=%fused_computation.15 | convolution fusion | flops 808976384 | bytes 1050624 | tf_op jit(solution)/shard_map/recb,keb->rck/dot_general | solution.py:43
  214.6 6.4 fusion.4
  221.0 6.0 fusion.5
  227.0 6.2 multiply_subtract_fusion
  233.2 5.6 fusion.13
  238.9 7.0 fusion.15
  245.9 5.7 fusion.2
  253.2 9.7 %fusion.3 = f32[4,16,64,32]{2,3,0,1:T(8,128)} fusion(f32[16,32,4,64]{3,1,2,0:T(8,128)} %fusion.15, f32[4,64,512]{2,1,0:T(8,128)S(1)} %copy-done.9, s32[16,32]{1,0:T(8,128)S(1)} %multiply_add_fusion.3), kind=kOutput, calls=%fused_computation.12 | convolution fusion | flops 809107456 | bytes 1574912 | tf_op jit(solution)/shard_map/rck,keb->recb/dot_general | solution.py:105
  262.9 1.8 copy.54
  265.9 49.3 %copy.56 = f32[2,4,1,32768]{1,2,0,3:T(1,128)} copy(f32[2,4,1,32768]{3,1,2,0:T(4,128)S(1)} %pad_maximum_fusion.2) | data formatting | bytes 2097152 | tf_op jit(solution)/shard_map/stack | solution.py:111
  315.8 123.9 %reduce = f32[32768,2,4]{2,1,0:T(2,128)} reduce(f32[32768,2,1,4]{3,2,1,0:T(1,128)} %bitcast.164, f32[]{:T(128)} %broadcast.181), dimensions={2}, to_apply=%bitcast.143.reduce_sub_computation | reduce | bytes 2097156
  439.7 53.1 %reshape.135 = f32[16,1,16384]{2,1,0:T(1,128)} reshape(f32[32768,2,4]{2,1,0:T(2,128)} %reduce) | data formatting | bytes 2097152
  492.7 6.9 all-to-all-start.4
  500.4 22.5 %all-to-all-done.4 = f32[16,1,16384]{2,1,0:T(1,128)S(1)} async-done(((f32[16,1,16384]{2,1,0:T(1,128)}), f32[16,1,16384]{2,1,0:T(1,128)S(1)}, u32[]{:S(2)}, u32[]{:S(2)}) %all-to-all-start.4) | async-done | bytes 1048608 | tf_op jit(solution)/shard_map/all_to_all | solution.py:112
  522.8 3.1 reduce.1
  526.0 74.9 %reshape.136 = f32[32768,2,1,4]{3,2,1,0:T(1,128)} reshape(f32[16,16384]{1,0:T(8,128)S(1)} %reduce.1) | data formatting | bytes 2097152
  600.9 22.7 %fusion.174 = (f32[1,4,1,32768]{1,2,0,3:T(1,128)}, f32[1,4,1,32768]{1,2,0,3:T(1,128)}) fusion(f32[2,4,1,32768]{1,2,0,3:T(1,128)} %bitcast.165), kind=kLoop, calls=%fused_computation.194 | loop fusion | bytes 2097152 | tf_op jit(solution)/shard_map/slice | solution.py:117
  623.6 29.8 %copy.58 = f32[1,4,1,32768]{3,1,2,0:T(4,128)S(1)} copy(f32[1,4,1,32768]{1,2,0,3:T(1,128)} %get-tuple-element.6) | data formatting | bytes 1048576 | tf_op jit(solution)/shard_map/slice | solution.py:117
  653.8 30.1 %copy.57 = f32[1,4,1,32768]{3,1,2,0:T(4,128)S(1)} copy(f32[1,4,1,32768]{1,2,0,3:T(1,128)} %get-tuple-element.5) | data formatting | bytes 1048576 | tf_op jit(solution)/shard_map/slice | solution.py:117
  684.3 2.6 fusion.38
  686.9 2.6 fusion.1
  689.8 14.7 %all_to_all.72 = f32[32,1,2048]{2,1,0:T(1,128)S(1)} all-to-all(f32[32,1,2048]{2,1,0:T(1,128)S(1)} %copy.59), channel_id=1, replica_groups=mesh['ctx'=16,'ch'=2] {'ctx'}, dimensions={0} | all-to-all | bytes 524288 | tf_op jit(solution)/shard_map/all_to_all | solution.py:123
  705.7 2.0 all_gather.10
  707.7 7.0 convolution_convert_fusion
  (69 shorter events, 16.5 us)
Async XLA Ops:
  6.5 74.2 %all-gather.3.cloned.1.call-start = ((), (), s32[]{:S(2)}) async-start(), calls=%async_computation.7 | async-start | bytes 3342336 | tf_op jit(solution)/shard_map/all_gather | solution.py:60
  7.3 100.9 %reduce-scatter.2.cloned.1.call-start = ((), (), s32[]{:S(2)}) async-start(), calls=%async_computation.8 | async-start | bytes 2359296 | tf_op jit(solution)/shard_map/reduce_scatter | solution.py:63
  93.3 7.1 copy-start.4
  102.2 13.5 %all-to-all-start.2 = ((f32[2,16,2048]{2,0,1:T(2,128)}), f32[2,16,2048]{2,0,1:T(2,128)S(1)}, u32[]{:S(2)}, u32[]{:S(2)}) async-start(f32[2,16,2048]{2,0,1:T(2,128)} %reshape.134), calls=%async_computation.3 | async-start | bytes 524288 | tf_op jit(solution)/shard_map/all_to_all | solution.py:85
  111.4 18.8 %copy-start.5 = (s32[32]{0:T(128)S(1)}, s32[32]{0:T(128)}, u32[]{:S(2)}) copy-start(s32[32]{0:T(128)} %param.10) | copy-start | bytes 388
  115.8 14.2 %all-to-all-start = ((f32[2,16,2048]{2,0,1:T(2,128)}), f32[2,16,2048]{2,0,1:T(2,128)S(1)}, u32[]{:S(2)}, u32[]{:S(2)}) async-start(f32[2,16,2048]{2,0,1:T(2,128)} %reshape.133), calls=%async_computation.1 | async-start | bytes 524288 | tf_op jit(solution)/shard_map/all_to_all | solution.py:93
  136.4 27.5 %all-to-all-start.3 = ((f32[2,4,16,2048]{3,1,0,2:T(4,128)}), f32[2,4,16,2048]{3,1,0,2:T(4,128)S(1)}, u32[]{:S(2)}, u32[]{:S(2)}) async-start(f32[2,4,16,2048]{3,1,0,2:T(4,128)} %pad_maximum_fusion.1), calls=%async_computation.4 | async-start | bytes 2097152 | tf_op jit(solution)/shard_map/all_to_all | solution.py:86
  163.9 32.5 %all-to-all-start.1 = ((f32[2,4,16,2048]{3,1,0,2:T(4,128)}), f32[2,4,16,2048]{3,1,0,2:T(4,128)S(1)}, u32[]{:S(2)}, u32[]{:S(2)}) async-start(f32[2,4,16,2048]{3,1,0,2:T(4,128)} %pad_maximum_fusion), calls=%async_computation.2 | async-start | bytes 2097152 | tf_op jit(solution)/shard_map/all_to_all | solution.py:94
  175.0 7.7 %copy-start.1 = (f32[4,16,64,32]{3,2,1,0:T(8,128)S(1)}, f32[4,16,64,32]{3,2,1,0:T(8,128)}, u32[]{:S(2)}) copy-start(f32[4,16,64,32]{3,2,1,0:T(8,128)} %squeeze.29) | copy-start | bytes 1572868
  206.8 7.7 %copy-start.2 = (f32[4,16,64,32]{3,2,1,0:T(8,128)S(1)}, f32[4,16,64,32]{3,2,1,0:T(8,128)}, u32[]{:S(2)}) copy-start(f32[4,16,64,32]{3,2,1,0:T(8,128)} %squeeze.26) | copy-start | bytes 1572868
  206.8 7.7 %copy-start.11 = (f32[4,64,512]{2,1,0:T(8,128)S(1)}, f32[4,64,512]{2,1,0:T(8,128)}, u32[]{:S(2)}) copy-start(f32[4,64,512]{2,1,0:T(8,128)} %convolution_bitcast_fusion.6) | copy-start | bytes 1572868
  214.5 6.4 copy-start
  214.6 6.4 copy-start.10
  221.0 6.0 copy-start.7
  233.2 5.6 copy-start.8
  252.1 1.0 copy-start.9
  492.7 30.1 %all-to-all-start.4 = ((f32[16,1,16384]{2,1,0:T(1,128)}), f32[16,1,16384]{2,1,0:T(1,128)S(1)}, u32[]{:S(2)}, u32[]{:S(2)}) async-start(f32[16,1,16384]{2,1,0:T(1,128)} %reshape.135), calls=%async_computation.5 | async-start | bytes 2097152 | tf_op jit(solution)/shard_map/all_to_all | solution.py:112
  499.6 208.1 %all-gather.5.cloned.1.call-start = ((), (), s32[]{:S(2)}) async-start(), calls=%async_computation.9 | async-start | bytes 1114112 | tf_op jit(solution)/shard_map/all_gather | solution.py:133
  704.5 1.0 copy-start.3
  704.5 1.0 copy-start.6
Sparse Core Ops, SparseCore 0:
  10.1 70.5 all-gather.2
  100.5 7.6 reduce-scatter.1
  503.2 58.3 all-gather.4
where the time goes:
time: 730 us; the launch traced here: 722 us
  local copies, waits for them, and re-layouts  295 us (40%)
  waiting for transfers between devices  133 us (18%)
  other arithmetic  131 us (18%)
  matrix products  107 us (15%)
  starting transfers between devices  25.2 us (3%)
  blocking collectives  16.7 us (2%)
  between operations  14.1 us (2%)
    unnamed x28, local copies, waits for them, and re-layouts  129 us
    unnamed x1, other arithmetic  124 us
    slice x3, local copies, waits for them, and re-layouts, per_device(): turned_real = returned[0] * cos_phi - returned[1] * sin_phi  82.6 us
    all_gather x1, waiting for transfers between devices, per_device(): weights_all = lax.all_gather(in_weight, 'ctx', axis=0, tiled=True)  73.4 us
    another operation x3, local copies, waits for them, and re-layouts, per_device(): jnp.stack([back_real, back_imag]).reshape(2, 4, 1, ctx_count * width)  51.2 us
    all_to_all x1, waiting for transfers between devices, per_device(): lax.all_to_all(stacked, 'ctx', split_axis=3, concat_axis=2, tiled=True)  22.5 us
    all_to_all x1, waiting for transfers between devices, per_device(): lax.all_to_all(block_section(filter_recv, theta_filter, phi, ctx_count),...  21.9 us
    dot_general x2, matrix products, freq_section(): jnp.einsum('recb,keb->rck', real_in, sin_b, precision=highest)  15.4 us
  transfers between devices with their start and end apart: 8, of which 6 were waited for; matrix products, arithmetic and copies ran while one was open for 28% of the time, Pallas kernels for 0%

commit v1 on v0

v1 whole, which is shorter than its diff:
```python
import math

import jax
import jax.numpy as jnp
from jax import lax
from jax.sharding import PartitionSpec as P

high = lax.Precision.HIGH


def split_length(length):
    cols = 1 << ((length.bit_length() - 1) // 2)
    return length // cols, cols


def cos_sin(numer, period):
    angle = (numer % period).astype(jnp.float32) * (2.0 * math.pi / period)
    return jnp.cos(angle), jnp.sin(angle)


def row_table(row_ids, rows):
    freq = 4 * jnp.arange(rows, dtype=jnp.int32) + 1
    cos, sin = cos_sin(freq[:, None] * row_ids[None, :], 4 * rows)
    return jnp.concatenate([cos, -sin], axis=0)


def col_table(cols):
    ids = jnp.arange(cols, dtype=jnp.int32)
    cos, sin = cos_sin(ids[:, None] * ids[None, :], cols)
    top = jnp.concatenate([cos, -sin], axis=1)
    bottom = jnp.concatenate([sin, cos], axis=1)
    return jnp.concatenate([top, bottom], axis=0)


def twist(rows, cols):
    freq = 4 * jnp.arange(rows, dtype=jnp.int32) + 1
    return cos_sin(freq[:, None] * jnp.arange(cols, dtype=jnp.int32)[None, :], 4 * rows * cols)


def spectrum(values, row_dft, col_dft, tw):
    rows, chans, cols = values.shape
    cos, sin = tw[0][:, None, :], tw[1][:, None, :]
    part = jnp.dot(row_dft, values.reshape(rows, chans * cols), precision=high)
    real = part[:rows].reshape(rows, chans, cols)
    imag = part[rows:].reshape(rows, chans, cols)
    turned = jnp.concatenate([real * cos + imag * sin, imag * cos - real * sin], axis=2)
    out = jnp.dot(turned.reshape(rows * chans, 2 * cols), col_dft, precision=high)
    return out.reshape(rows, chans, 2 * cols)


def causal_conv(values, taps, row_ids):
    rows, chans, cols = values.shape
    col_dft = col_table(cols)
    tw = twist(rows, cols)
    perm_dft = row_table(row_ids, rows)
    sig = spectrum(values, perm_dft, col_dft, tw)
    fil = spectrum(taps, row_table(jnp.arange(rows, dtype=jnp.int32), rows), col_dft, tw)
    sr, si = sig[..., :cols], sig[..., cols:]
    fr, fi = fil[..., :cols], fil[..., cols:]
    both = jnp.concatenate([sr * fr - si * fi, sr * fi + si * fr], axis=2)
    back = jnp.dot(both.reshape(rows * chans, 2 * cols), col_dft.T, precision=high)
    back = back.reshape(rows, chans, 2 * cols) * (1.0 / (rows * cols))
    br, bi = back[..., :cols], back[..., cols:]
    cos, sin = tw[0][:, None, :], tw[1][:, None, :]
    turned = jnp.concatenate([br * cos - bi * sin, br * sin + bi * cos], axis=0)
    out = jnp.dot(perm_dft.T, turned.reshape(2 * rows, chans * cols), precision=high)
    return out.reshape(rows, chans, cols)


def per_device(tokens, in_weight, conv_filter, skip_gain, group_order, out_weight):
    ctx = lax.axis_size("ctx")
    ch = lax.axis_size("ch")
    tok_count, feat_local = tokens.shape
    chan_local = conv_filter.shape[0]
    seq = tok_count * ctx
    group = seq // group_order.shape[0]
    rows, cols = split_length(seq)
    own_rows = tok_count // cols
    owned = -(-chan_local // ctx)
    padded = owned * ctx

    def outward(signal):
        signal = jnp.pad(signal, ((0, padded - chan_local), (0, 0)))
        parts = signal.reshape(ctx, owned, own_rows, cols).transpose(0, 2, 1, 3)
        got = lax.all_to_all(parts, "ctx", split_axis=0, concat_axis=0, tiled=True)
        return got.reshape(rows, owned, cols)

    taps = outward(conv_filter)
    mine = in_weight.reshape(-1, feat_local)
    flat = lax.all_gather(mine, "ctx", axis=0, tiled=True)
    partial = lax.dot_general(flat, tokens, (((1,), (1,)), ((), ())), preferred_element_type=jnp.float32)
    if ch == 2:
        me = lax.axis_index("ch")
        half = partial.shape[0] // 2
        away = lax.dynamic_slice_in_dim(partial, (1 - me) * half, half, 0)
        kept = lax.dynamic_slice_in_dim(partial, me * half, half, 0)
        proj = kept + lax.ppermute(away, "ch", [(0, 1), (1, 0)])
    else:
        proj = lax.psum_scatter(partial, "ch", scatter_dimension=0, tiled=True)
    proj = proj.reshape(chan_local, 3, tok_count)
    gate = proj[:, 0]
    product = proj[:, 1] * proj[:, 2]
    in_group = jnp.arange(group // cols, dtype=jnp.int32)
    row_ids = (group_order[:, None] * (group // cols) + in_group[None, :]).reshape(rows)
    conv = causal_conv(outward(product), taps, row_ids)
    back = lax.all_to_all(
        conv.reshape(ctx, own_rows, owned, cols), "ctx", split_axis=0, concat_axis=0, tiled=True
    )
    conv = back.transpose(0, 2, 1, 3).reshape(padded, tok_count)[:chan_local]
    hidden = (gate * (conv + skip_gain[:, None] * product)).astype(jnp.bfloat16)
    hidden_all = lax.all_gather(hidden, "ch", axis=0, tiled=True)
    rows_all = lax.all_gather(out_weight, "ctx", axis=0, tiled=True)
    mixed = lax.dot_general(
        hidden_all, rows_all, (((0,), (0,)), ((), ())), preferred_element_type=jnp.float32
    )
    return mixed.astype(jnp.bfloat16)


def solution(mesh):
    in_specs = (P("ctx", "ch"), P("ctx", None, "ch"), P("ch", "ctx"), P("ch"), P(), P("ctx", "ch"))
    return jax.shard_map(
        per_device, mesh=mesh, in_specs=in_specs, out_specs=P("ctx", "ch"), check_vma=False
    )
```

time: 730 us -> 155 us (0.21); the launches traced: 722 us -> 154 us
  local copies, waits for them, and re-layouts: 295 us -> 5.09 us
  other arithmetic: 131 us -> 6.27 us
  matrix products: 107 us -> 17 us
  waiting for transfers between devices: 133 us -> 83.7 us
  starting transfers between devices: 25.2 us -> 12.6 us
    unnamed x28 -> x19, local copies, waits for them, and re-layouts: 129 us -> 2.88 us
    unnamed x1 -> x0, other arithmetic: 124 us -> none
    dot_general x18 -> x6, matrix products: 92.7 us -> 3.17 us  [the longest x2 1.59 us: spectrum(): part = jnp.dot(row_dft, values.reshape(rows, chans * cols), precision=high)]
    slice x9 -> x3, local copies, waits for them, and re-layouts: 84.1 us -> 0.28 us  [the longest x2 0.16 us: spectrum(): imag = part[rows:].reshape(rows, chans, cols)]
    another operation x7 -> x0, local copies, waits for them, and re-layouts: 52.6 us -> none  [the longest x3 51.2 us: per_device(): jnp.stack([back_real, back_imag]).reshape(2, 4, 1, ctx_count * width)]
    all_to_all x5 -> x2, waiting for transfers between devices: 56.7 us -> 8.8 us  [outward(): got = lax.all_to_all(parts, 'ctx', split_axis=0, concat_axis=0, tiled=True)]
    all_to_all x5 -> x2, starting transfers between devices: 25.2 us -> 12.5 us  [outward(): got = lax.all_to_all(parts, 'ctx', split_axis=0, concat_axis=0, tiled=True)]
    all_gather x1, waiting for transfers between devices: 0.01 us -> 12.5 us  [per_device(): rows_all = lax.all_gather(out_weight, 'ctx', axis=0, tiled=True)]
  transfers between devices with their start and end apart: 8 -> 5, of which waited for: 6 -> 3; matrix products, arithmetic and copies ran while one was open for 28% -> 13% of each run, Pallas kernels for 0% -> 0%
where the time goes in v1:
time: 155 us; the launch traced here: 154 us
  waiting for transfers between devices  83.7 us (54%)
  matrix products  17 us (11%)
  blocking collectives  15.7 us (10%)
  between operations  13.7 us (9%)
  starting transfers between devices  12.6 us (8%)
  other arithmetic  6.27 us (4%)
  local copies, waits for them, and re-layouts  5.09 us (3%)
    all_gather x1, waiting for transfers between devices, per_device(): flat = lax.all_gather(mine, 'ctx', axis=0, tiled=True)  61.7 us
    all_to_all x1, blocking collectives, per_device(): lax.all_to_all(conv.reshape(ctx, own_rows, owned, cols), 'ctx', split_axi...  13.7 us
    all_gather x1, waiting for transfers between devices, per_device(): rows_all = lax.all_gather(out_weight, 'ctx', axis=0, tiled=True)  12.5 us
    all_to_all x2, starting transfers between devices, outward(): got = lax.all_to_all(parts, 'ctx', split_axis=0, concat_axis=0, tiled=True)  12.5 us
    all_to_all x2, waiting for transfers between devices, outward(): got = lax.all_to_all(parts, 'ctx', split_axis=0, concat_axis=0, tiled=True)  8.8 us
    dot_general x1, matrix products, per_device(): lax.dot_general(hidden_all, rows_all, (((0,), (0,)), ((), ())), preferred...  6.99 us
    dot_general x1, matrix products, per_device(): lax.dot_general(flat, tokens, (((1,), (1,)), ((), ())), preferred_element...  6.84 us
  transfers between devices with their start and end apart: 5, of which 3 were waited for; matrix products, arithmetic and copies ran while one was open for 13% of the time, Pallas kernels for 0%

profile of v1, /device:TPU:0, one launch (start us, length us, event | category | flops | bytes accessed | tf_op | source)
XLA Modules:
  0.0 154.1 jit_solution(13699279808950196309)
XLA Ops:
  6.5 0.0 all-gather.3.cloned.1.call-start
  6.5 1.1 copy.13
  7.6 0.8 reshape.145
  8.5 0.0 all-gather.3.cloned.1.call-update
  8.5 1.7 %copy.32 = f32[8,8,8,128]{3,2,1,0:T(8,128)} copy(f32[8,8,8,128]{3,1,2,0:T(8,128)} %bitcast.81) | data formatting | bytes 524288
  10.2 8.3 %all-to-all-start.1 = ((f32[16,8,4,128]{3,1,2,0:T(8,128)}), f32[16,8,4,128]{3,1,2,0:T(8,128)S(1)}, u32[]{:S(2)}, u32[]{:S(2)}) async-start(f32[16,8,4,128]{3,1,2,0:T(8,128)} %bitcast.9), calls=%async_computation.1 | async-start | bytes 524288 | tf_op jit(solution)/shard_map/all_to_all | solution.py:85
  18.6 0.0 all-gather.5.cloned.1.call-start
  18.6 0.7 all-gather.5.cloned.1.call-update
  19.3 0.7 broadcast_multiply_fusion
  20.0 61.7 %all-gather.3.cloned.1.call-done = bf16[384,4096]{1,0:T(8,128)(2,1)} async-done(((bf16[24,4096]{1,0:T(8,128)(2,1)}), bf16[384,4096]{1,0:T(8,128)(2,1)}) %all-gather.3.cloned.1.call-update) | async-done | bytes 3145744 | tf_op jit(solution)/shard_map/all_gather | solution.py:90
  81.7 6.8 %fusion.60 = f32[384,1024]{1,0:T(8,128)S(1)} fusion(bf16[384,4096]{1,0:T(8,128)(2,1)} %all-gather.3.cloned.1.call-done, bf16[1024,4096]{1,0:T(8,128)(2,1)} %param.6), kind=kOutput, calls=%fused_computation.102 | convolution fusion | flops 3221225472 | bytes 13107200 | tf_op jit(solution)/shard_map/dot_general | solution.py:91
  88.6 0.1 constant_dynamic-slice_fusion
  88.7 0.1 collective-permute-start
  88.7 0.1 iota_add_fusion
  88.8 0.1 add.147
  88.9 0.3 fusion.46
  89.2 1.5 fusion.51
  90.7 0.7 fusion.25
  91.4 0.0 copy-done
  91.4 0.0 collective-permute-done
  91.4 0.1 dynamic-slice_add_fusion
  91.6 0.3 reshape.146
  91.9 1.2 fusion.58
  93.2 0.0 all-to-all-done.1
  93.2 4.2 %all-to-all-start = ((f32[16,8,4,128]{3,1,2,0:T(8,128)}), f32[16,8,4,128]{3,1,2,0:T(8,128)S(1)}, u32[]{:S(2)}, u32[]{:S(2)}) async-start(f32[16,8,4,128]{3,1,2,0:T(8,128)} %bitcast.6), calls=%async_computation | async-start | bytes 524288 | tf_op jit(solution)/shard_map/all_to_all | solution.py:85
  97.3 0.3 fusion.52
  97.6 0.1 copy.15
  97.7 1.2 fusion.17
  99.0 0.1 copy.22
  99.1 0.1 copy.23
  99.3 0.1 copy.20
  99.4 0.1 copy.21
  99.5 8.8 %all-to-all-done = f32[16,8,4,128]{3,1,2,0:T(8,128)S(1)} async-done(((f32[16,8,4,128]{3,1,2,0:T(8,128)}), f32[16,8,4,128]{3,1,2,0:T(8,128)S(1)}, u32[]{:S(2)}, u32[]{:S(2)}) %all-to-all-start) | async-done | bytes 262176 | tf_op jit(solution)/shard_map/all_to_all | solution.py:85
  108.3 0.4 fusion.19
  108.8 0.1 fusion.15
  108.9 0.4 fusion
  109.3 0.4 fusion.4
  109.7 0.1 multiply_subtract_fusion.1
  109.8 0.0 copy-start.7
  109.8 0.4 convolution_multiply_fusion
  110.2 0.1 multiply_subtract_fusion
  110.3 0.2 copy.26
  110.5 0.4 fusion.11
  110.9 13.7 %all_to_all.15 = f32[16,8,4,128]{3,1,2,0:T(8,128)S(1)} all-to-all(f32[16,8,4,128]{3,1,2,0:T(8,128)S(1)} %fusion.11), channel_id=1, replica_groups=mesh['ctx'=16,'ch'=2] {'ctx'}, dimensions={0} | all-to-all | bytes 524288 | tf_op jit(solution)/shard_map/all_to_all | solution.py:106
  124.6 1.1 fusion.14
  125.8 2.0 %all_gather.10 = bf16[128,1024]{1,0:T(8,128)(2,1)S(1)} all-gather(bf16[64,1024]{1,0:T(8,128)(2,1)S(1)} %fusion.14), channel_id=1, replica_groups=mesh['ctx'=16,'ch'=2] {'ch'}, dimensions={0}, use_global_device_ids=true | all-gather | bytes 393216 | tf_op jit(solution)/shard_map/all_gather | solution.py:111
  127.8 12.5 %all-gather.5.cloned.1.call-done = bf16[128,4096]{1,0:T(8,128)(2,1)} async-done(((bf16[8,4096]{1,0:T(8,128)(2,1)}), bf16[128,4096]{1,0:T(8,128)(2,1)}) %all-gather.5.cloned.1.call-update) | async-done | bytes 1048592 | tf_op jit(solution)/shard_map/all_gather | solution.py:112
  140.3 7.0 %convolution_convert_fusion = bf16[1024,4096]{1,0:T(8,128)(2,1)} fusion(bf16[128,1024]{1,0:T(8,128)(2,1)S(1)} %all_gather.10, bf16[128,4096]{1,0:T(8,128)(2,1)} %all-gather.5.cloned.1.call-done), kind=kOutput, calls=%fused_computation | convolution fusion | flops 1077936128 | bytes 9699328 | tf_op jit(solution)/shard_map/dot_general | solution.py:113
  (18 shorter events, 0.1 us)
Async XLA Ops:
  6.5 75.2 %all-gather.3.cloned.1.call-start = ((), (), s32[]{:S(2)}) async-start(), calls=%async_computation.3 | async-start | bytes 3342336 | tf_op jit(solution)/shard_map/all_gather | solution.py:90
  10.2 82.9 %all-to-all-start.1 = ((f32[16,8,4,128]{3,1,2,0:T(8,128)}), f32[16,8,4,128]{3,1,2,0:T(8,128)S(1)}, u32[]{:S(2)}, u32[]{:S(2)}) async-start(f32[16,8,4,128]{3,1,2,0:T(8,128)} %bitcast.9), calls=%async_computation.1 | async-start | bytes 524288 | tf_op jit(solution)/shard_map/all_to_all | solution.py:85
  18.6 121.7 %all-gather.5.cloned.1.call-start = ((), (), s32[]{:S(2)}) async-start(), calls=%async_computation.4 | async-start | bytes 1114112 | tf_op jit(solution)/shard_map/all_gather | solution.py:112
  88.7 2.8 %collective-permute-start = (f32[192,1024]{1,0:T(8,128)S(1)}, f32[192,1024]{1,0:T(8,128)S(1)}, u32[]{:S(2)}, u32[]{:S(2)}) collective-permute-start(f32[192,1024]{1,0:T(8,128)S(1)} %constant_dynamic-slice_fusion), channel_id=1, source_target_pairs={{0,1},{1,0},{2,3},{3,2},{4,5},{5,4},{6,7},{7,6},{8,9},{9,8},{10,11... | collective-permute-start | bytes 2359304 | tf_op jit(solution)/shard_map/ppermute | solution.py:97
  90.7 0.7 copy-start
  90.7 0.7 copy-start.2
  91.6 6.0 %copy-start.6 = (f32[128,256]{0,1:T(8,128)S(1)}, f32[128,256]{0,1:T(8,128)}, u32[]{:S(2)}) copy-start(f32[128,256]{0,1:T(8,128)} %fusion.25) | copy-start | bytes 393220
  91.9 16.4 %copy-start.1 = (f32[128,128]{1,0:T(8,128)S(1)}, f32[128,128]{1,0:T(8,128)}, u32[]{:S(2)}) copy-start(f32[128,128]{1,0:T(8,128)} %copy-done) | copy-start | bytes 196612
  91.9 16.4 %copy-start.3 = (f32[128,128]{1,0:T(8,128)S(1)}, f32[128,128]{1,0:T(8,128)}, u32[]{:S(2)}) copy-start(f32[128,128]{1,0:T(8,128)} %copy-done.2) | copy-start | bytes 196612
  93.2 15.2 %all-to-all-start = ((f32[16,8,4,128]{3,1,2,0:T(8,128)}), f32[16,8,4,128]{3,1,2,0:T(8,128)S(1)}, u32[]{:S(2)}, u32[]{:S(2)}) async-start(f32[16,8,4,128]{3,1,2,0:T(8,128)} %bitcast.6), calls=%async_computation | async-start | bytes 524288 | tf_op jit(solution)/shard_map/all_to_all | solution.py:85
  97.6 11.2 %copy-start.4 = (f32[128,128]{1,0:T(8,128)S(1)}, f32[128,128]{1,0:T(8,128)}, u32[]{:S(2)}) copy-start(f32[128,128]{1,0:T(8,128)} %get-tuple-element.23) | copy-start | bytes 196612
  97.6 11.2 %copy-start.5 = (f32[128,128]{1,0:T(8,128)S(1)}, f32[128,128]{1,0:T(8,128)}, u32[]{:S(2)}) copy-start(f32[128,128]{1,0:T(8,128)} %get-tuple-element.26) | copy-start | bytes 196612
  109.8 14.9 %copy-start.7 = (f32[64]{0:T(128)S(1)}, f32[64]{0:T(128)}, u32[]{:S(2)}) copy-start(f32[64]{0:T(128)} %param.9) | copy-start | bytes 772
Sparse Core Ops, SparseCore 0:
  10.1 71.5 all-gather.2
  84.5 55.7 all-gather.4
